TPU v7x, 32 devices: a whole 2x2x4 slice. The times are simulated.
32 devices in a mesh: tok: 8 (over z, y), exp: 4 (over x, core).
Axes of the slice: x: 2, y: 2, z: 4, core: 2. Of those that a mesh axis runs over, the one named last changes fastest.
Arguments:
- tokens: bfloat16 [12, 8192, 1024], P(None, 'tok'), may hold values from -24 to 24
- slot_params: bfloat16 [1024, 128], P(None, 'exp'), may hold values from -2 to 2
- w_in: bfloat16 [64, 1024, 4096], P('exp', None, 'tok'), may hold values from -0.75 to 0.75
- w_out: bfloat16 [64, 4096, 1024], P('exp', 'tok'), may hold values from -0.1875 to 0.1875
Outputs:
- mixed: bfloat16 [12, 8192, 1024], P(None, 'tok', 'exp')
All inputs are finite; a program needn't handle non-finite values.
Results may differ from a plain program's by a relative error of at most 0.0072.
Values may be sent and summed in bfloat16 or wider, within the bound.
A program may use at most 192 MiB of HBM per device.

v0:
```python
import jax
import jax.numpy as jnp
from jax import lax
from jax.sharding import PartitionSpec as P

SLOTS_PER = 2


def shards(tokens, slot_params, w_in, w_out):
    own_width = slot_params.shape[1]
    own_logits = jnp.einsum("std,dj->sjt", tokens, slot_params, preferred_element_type=jnp.float32)
    all_logits = lax.all_gather(own_logits, "exp", axis=1, tiled=True)
    local_max = jnp.max(own_logits, axis=2)
    slot_peak = lax.pmax(local_max, "tok")
    dexp = jnp.exp(own_logits - slot_peak[:, :, None])
    local_den = jnp.sum(dexp, axis=2)
    dweight = dexp.astype(jnp.bfloat16)
    local_sum = jnp.einsum("sjt,std->sjd", dweight, tokens, preferred_element_type=jnp.float32)
    slot_sum, slot_den = lax.psum((local_sum, local_den), "tok")
    slot_in = (slot_sum / slot_den[:, :, None]).astype(jnp.bfloat16)
    seq_count = tokens.shape[0]
    local_experts = w_in.shape[0]
    width = tokens.shape[2]
    grouped = slot_in.reshape(seq_count, local_experts, SLOTS_PER, width)
    hidden = jax.nn.gelu(
        jnp.einsum("sepd,edf->sepf", grouped, w_in, preferred_element_type=jnp.float32),
        approximate=True,
    ).astype(jnp.bfloat16)
    partial_out = jnp.einsum("sepf,efd->sepd", hidden, w_out, preferred_element_type=jnp.float32)
    partial_out = partial_out.reshape(seq_count, own_width, width)
    summed = lax.psum(partial_out, "tok").astype(jnp.bfloat16)
    slot_out = lax.all_to_all(summed, "exp", split_axis=2, concat_axis=1, tiled=True)
    comb_max = jnp.max(all_logits, axis=1)
    cexp = jnp.exp(all_logits - comb_max[:, None, :])
    cweight = (cexp / jnp.sum(cexp, axis=1)[:, None, :]).astype(jnp.bfloat16)
    mixed = jnp.einsum("sjt,sjd->std", cweight, slot_out, preferred_element_type=jnp.float32)
    return mixed.astype(jnp.bfloat16)


def solution(mesh):
    return jax.shard_map(
        shards,
        mesh=mesh,
        in_specs=(
            P(None, "tok", None),
            P(None, "exp"),
            P("exp", None, "tok"),
            P("exp", "tok", None),
        ),
        out_specs=P(None, "tok", "exp"),
        check_vma=False,
    )
```

profile of v0, /device:TPU:0, one launch (start us, length us, event | category | flops | bytes accessed | tf_op | source)
XLA Modules:
  0.0 546.4 jit_solution(2624365932778062341)
XLA Ops:
  7.4 0.0 copy-start
  7.4 0.0 all-reduce.3.cloned.1.call-start
  7.4 0.8 copy-done
  8.2 12.3 %fusion.28 = (f32[12,32]{1,0:T(8,128)S(1)}, f32[12,32,1024]{2,1,0:T(8,128)S(1)}) fusion(bf16[12,1024,1024]{2,1,0:T(8,128)(2,1)} %param.4, bf16[1024,32]{0,1:T(8,128)(2,1)S(1)} %copy-done), kind=kOutput, calls=%fused_computation.28 | convolution fusion | flops 805699200 | bytes 26805760 | tf_op jit(solution)/shard_map/std,dj->sjt/dot_general | solution.py:11
  20.5 0.0 copy-start.2
  20.5 23.4 %pmax.7 = f32[12,32]{1,0:T(8,128)S(1)} all-reduce(f32[12,32]{1,0:T(8,128)S(1)} %get-tuple-element.5), channel_id=1, replica_groups=mesh['tok'=8,'exp'=4] {'tok'}, use_global_device_ids=true, to_apply=%region_3.0 | all-reduce | flops 384 | bytes 3072 | tf_op jit(solution)/shard_map/pmax | solution.py:14
  43.9 11.7 %fusion.23 = f32[12,32,1024]{2,1,0:T(8,128)} fusion(bf16[12,1024,1024]{2,1,0:T(8,128)(2,1)} %param.4, f32[12,32,1024]{2,1,0:T(8,128)S(1)} %get-tuple-element.6, f32[12,32]{1,0:T(8,128)S(1)} %pmax.7), kind=kOutput, calls=%fused_computation.24 | convolution fusion | flops 806092800 | bytes 28313088 | tf_op jit(solution)/shard_map/sjt,std->sjd/dot_general | solution.py:18
  55.6 0.0 copy-done.2
  55.6 0.0 all-reduce.3.cloned.1.call-update
  55.6 0.0 all-gather.2.cloned.1.call-start
  55.6 0.5 all-gather.2.cloned.1.call-update
  56.2 1.8 fusion.6
  57.9 18.4 %psum.22 = f32[12,32]{1,0:T(8,128)S(1)} all-reduce(f32[12,32]{1,0:T(8,128)S(1)} %fusion.6), channel_id=1, replica_groups=mesh['tok'=8,'exp'=4] {'tok'}, use_global_device_ids=true, to_apply=%region_6.0 | all-reduce | flops 384 | bytes 3072 | tf_op jit(solution)/shard_map/psum | solution.py:19
  76.3 66.0 %all-reduce.3.cloned.1.call-done = f32[12,32,1024]{2,1,0:T(8,128)} async-done(((f32[12,32,1024]{2,1,0:T(8,128)}), f32[12,32,1024]{2,1,0:T(8,128)}) %all-reduce.3.cloned.1.call-update) | async-done | bytes 1572880 | tf_op jit(solution)/shard_map/psum | solution.py:19
  142.3 1.6 divide_convert_fusion.2
  144.0 0.4 copy.20
  144.4 8.7 %fusion.20 = bf16[12,16,2,512]{3,0,2,1:T(8,128)(2,1)S(1)} fusion(bf16[12,16,2,1024]{3,0,2,1:T(8,128)(2,1)S(1)} %bitcast.48, bf16[16,1024,512]{2,1,0:T(8,128)(2,1)} %param.6), kind=kOutput, calls=%fused_computation.23 | convolution fusion | flops 404422656 | bytes 17956864 | tf_op jit(solution)/shard_map/sepd,edf->sepf/dot_general | solution.py:26
  153.2 8.7 %fusion.1 = f32[16,12,2,1024]{3,1,2,0:T(8,128)S(1)} fusion(bf16[12,16,2,512]{3,0,2,1:T(8,128)(2,1)S(1)} %fusion.20, bf16[16,512,1024]{2,1,0:T(8,128)(2,1)} %param.7), kind=kOutput, calls=%fused_computation.1 | convolution fusion | flops 402653184 | bytes 18743296 | tf_op jit(solution)/shard_map/sepf,efd->sepd/dot_general | solution.py:29
  161.9 6.5 %copy.13 = f32[12,32,1024]{1,0,2:T(8,128)} copy(f32[12,32,1024]{2,0,1:T(8,128)S(1)} %bitcast.47) | data formatting | bytes 3145728 | tf_op jit(solution)/shard_map/reshape | solution.py:30
  168.4 326.7 %all-reduce.4 = bf16[12,32,1024]{1,0,2:T(8,128)(2,1)} all-reduce(f32[12,32,1024]{1,0,2:T(8,128)} %copy.13), channel_id=1, replica_groups=mesh['tok'=8,'exp'=4] {'tok'}, use_global_device_ids=true, to_apply=%region_7.0 | all-reduce | flops 393216 | bytes 2359296 | tf_op jit(solution)/shard_map/psum | solution.py:31
  495.1 5.0 reshape.15
  500.1 14.2 %all_to_all.18 = bf16[4,2,49152]{2,1,0:T(2,128)(2,1)S(1)} all-to-all(bf16[4,2,49152]{2,1,0:T(2,128)(2,1)S(1)} %reshape.15), channel_id=1, replica_groups=mesh['tok'=8,'exp'=4] {'exp'}, dimensions={0} | all-to-all | bytes 1572864 | tf_op jit(solution)/shard_map/all_to_all | solution.py:32
  514.3 4.1 reshape.16
  518.4 5.1 copy.21
  523.6 0.1 copy.15
  523.7 0.0 all-gather.2.cloned.1.call-done
  523.7 5.8 %fusion.29 = f32[12,1024]{1,0:T(8,128)S(1)} fusion(f32[12,128,1024]{2,1,0:T(8,128)} %all-gather.2.cloned.1.call-done), kind=kOutput, calls=%fused_computation.29 | output fusion | flops 3145855 | bytes 6340608 | tf_op jit(solution)/shard_map/sub | solution.py:34
  529.5 0.0 copy-start.1
  529.6 9.4 %convolution_convert_fusion = bf16[12,1024,256]{2,1,0:T(8,128)(2,1)} fusion(bf16[12,128,256]{2,1,0:T(8,128)(2,1)S(1)} %bitcast.50, f32[12,1024]{1,0:T(8,128)S(1)} %fusion.29, f32[12,128,1024]{2,1,0:T(8,128)} %all-gather.2.cloned.1.call-done), kind=kOutput, calls=%fused_computation.7 | convolution fusion | flops 813183104 | bytes 13418496 | tf_op jit(solution)/shard_map/sjt,sjd->std/dot_general | solution.py:36
  539.0 0.0 copy-done.1
Async XLA Ops:
  7.4 0.8 copy-start
  7.4 135.0 %all-reduce.3.cloned.1.call-start = ((), (), s32[]{:S(2)}) async-start(), calls=%async_computation.2 | async-start | bytes 3145728 | tf_op jit(solution)/shard_map/psum | solution.py:19
  20.5 35.0 %copy-start.2 = (f32[12,32,1024]{2,1,0:T(8,128)}, f32[12,32,1024]{2,1,0:T(8,128)S(1)}, u32[]{:S(2)}) copy-start(f32[12,32,1024]{2,1,0:T(8,128)S(1)} %get-tuple-element.6) | copy-start | bytes 4718596
  55.6 468.1 %all-gather.2.cloned.1.call-start = ((), (), s32[]{:S(2)}) async-start(), calls=%async_computation.1 | async-start | bytes 7864320 | tf_op jit(solution)/shard_map/all_gather | solution.py:12
  529.5 9.4 %copy-start.1 = (bf16[1024,32]{0,1:T(8,128)(2,1)S(1)}, bf16[1024,32]{0,1:T(8,128)(2,1)}, u32[]{:S(2)}) copy-start(bf16[1024,32]{0,1:T(8,128)(2,1)} %param.5) | copy-start | bytes 196612
Sparse Core Ops, SparseCore 0:
  55.7 86.5 all-reduce.2
Sparse Core Ops, SparseCore 1:
  57.6 43.5 all-gather.1
where the time goes:
time: 547 us; the launch traced here: 546 us
  blocking collectives  383 us (70%)
  waiting for transfers between devices  66.6 us (12%)
  matrix products  50.8 us (9%)
  local copies, waits for them, and re-layouts  22.2 us (4%)
  between operations  14.9 us (3%)
  other arithmetic  9.19 us (2%)
    psum x1, blocking collectives, shards(): summed = lax.psum(partial_out, 'tok').astype(jnp.bfloat16)  327 us
    psum x1, waiting for transfers between devices, shards(): slot_sum, slot_den = lax.psum((local_sum, local_den), 'tok')  66 us
    pmax x1, blocking collectives, shards(): slot_peak = lax.pmax(local_max, 'tok')  23.4 us
    psum x1, blocking collectives, shards(): slot_sum, slot_den = lax.psum((local_sum, local_den), 'tok')  18.4 us
    all_to_all x1, blocking collectives, shards(): lax.all_to_all(summed, 'exp', split_axis=2, concat_axis=1, tiled=True)  14.2 us
    dot_general x1, matrix products, shards(): jnp.einsum('std,dj->sjt', tokens, slot_params, preferred_element_type=jnp...  12.3 us
    dot_general x1, matrix products, shards(): jnp.einsum('sjt,std->sjd', dweight, tokens, preferred_element_type=jnp.fl...  11.7 us
  transfers between devices with their start and end apart: 2, of which 1 were waited for; matrix products, arithmetic and copies ran while one was open for 8% of the time, Pallas kernels for 0%

commit v1 on v0

--- a/solution.py
+++ b/solution.py
@@ -1,9 +1,322 @@
+import functools
+
 import jax
 import jax.numpy as jnp
 from jax import lax
+from jax.experimental import pallas as pl
+from jax.experimental.pallas import tpu as pltpu
 from jax.sharding import PartitionSpec as P
 
 SLOTS_PER = 2
+NZ, NY = 4, 2
+NT = NZ * NY
+NE = 4
+LANES = 128
+MESH = pl.DeviceIdType.MESH
+F32, BF16 = jnp.float32, jnp.bfloat16
+
+
+def gelu(v):
+    return 0.5 * v * (1.0 + jnp.tanh(0.7978845608 * (v + 0.044715 * (v * v * v))))
+
+
+def main_kernel(
+    tok_hbm, prm_ref, win_hbm, wout_hbm, cw_hbm, g_hbm,
+    tbuf, prm, win, wout, lg, cwbuf, part, psend, st, wrow, yrecv, zsend, zrecv, facc, xs,
+    acc, bsend, byrecv, bzsend, bzrecv, fin, g,
+    tsem, wsem, cwsem, gsem,
+    p_s, p_r, s_s, s_r, y_s, y_r, z_s, z_r, az_s, az_r, ay_s, ay_r,
+    by_s, by_r, bz_s, bz_r, c_s, c_r, gz_s, gz_r, gy_s, gy_r,
+):
+    seqs, _, width = tok_hbm.shape
+    own_w = prm_ref.shape[0]
+    pair_rows = acc.shape[0]
+    half_rows = pair_rows // 2
+    feat = g.shape[3]
+    t = lax.axis_index("tok")
+    e = lax.axis_index("exp")
+    z, y = t // NY, t % NY
+    oy = 1 - y
+    me = y * NZ + z
+
+    def remote(src, dst, ssem, rsem, tok, exp):
+        return pltpu.make_async_remote_copy(
+            src_ref=src, dst_ref=dst, send_sem=ssem, recv_sem=rsem,
+            device_id={"tok": tok, "exp": exp}, device_id_type=MESH)
+
+    def zpeer(d):
+        return lax.rem(z + d, NZ)
+
+    def tok_copy(s):
+        slot = lax.rem(s, 3)
+        return pltpu.make_async_copy(tok_hbm.at[s], tbuf.at[slot], tsem.at[slot])
+
+    def w_copies(p):
+        return (pltpu.make_async_copy(win_hbm.at[pl.ds(2 * p, 2)], win.at[pl.ds(2 * p, 2)], wsem.at[0, p]),
+                pltpu.make_async_copy(wout_hbm.at[pl.ds(2 * p, 2)], wout.at[pl.ds(2 * p, 2)], wsem.at[1, p]))
+
+    def cw_copy(s):
+        return pltpu.make_async_copy(cwbuf.at[s], cw_hbm.at[s], cwsem.at[s])
+
+    tok_copy(0).start()
+    tok_copy(1).start()
+
+    barrier = pltpu.get_barrier_semaphore()
+    for d in range(1, NT):
+        pl.semaphore_signal(barrier, inc=1, device_id={"tok": lax.rem(t + d, NT), "exp": e}, device_id_type=MESH)
+    for d in range(1, NE):
+        pl.semaphore_signal(barrier, inc=1, device_id={"tok": t, "exp": lax.rem(e + d, NE)}, device_id_type=MESH)
+    pl.semaphore_wait(barrier, NT + NE - 2)
+
+    own_cols = pl.ds(pl.multiple_of(e * own_w, own_w), own_w)
+    p_copies = [remote(prm_ref, prm.at[own_cols], p_s.at[d - 1], p_r.at[d - 1], t, lax.rem(e + d, NE)) for d in range(1, NE)]
+    for c in p_copies:
+        c.start()
+    prm[own_cols, :] = prm_ref[...]
+    st[me] = jnp.ones((own_w, LANES), F32)
+    for c in p_copies:
+        c.wait()
+
+    lane = lax.broadcasted_iota(jnp.int32, (own_w, LANES), 1)
+
+    def dispatch(s, carry):
+        @pl.when(s + 2 < seqs)
+        def _():
+            tok_copy(s + 2).start()
+
+        @pl.when(s < NT)
+        def _():
+            for c in w_copies(s):
+                c.start()
+
+        tok_copy(s).wait()
+        slot = lax.rem(s, 3)
+        logits = lax.dot_general(prm[...], tbuf[slot], (((1,), (1,)), ((), ())), preferred_element_type=F32)
+        lg[...] = logits
+        ex = jnp.exp(logits - jnp.max(logits, axis=0, keepdims=True))
+        cwbuf[s] = (ex / jnp.sum(ex, axis=0, keepdims=True)).astype(BF16)
+        cw_copy(s).start()
+        own = lg[own_cols, :]
+        peak = jnp.max(own, axis=1, keepdims=True)
+        dx = jnp.exp(own - peak)
+        den = jnp.sum(dx, axis=1, keepdims=True)
+        ssum = jnp.dot(dx.astype(BF16), tbuf[slot], preferred_element_type=F32)
+        scaled = ssum / den
+        for k in range(NT):
+            part[k, pl.ds(s, own_w, stride=seqs), :] = scaled[:, k * LANES:(k + 1) * LANES]
+        st[me] = jnp.where(lane == s, peak, jnp.where(lane == s + 64, den, st[me]))
+        return carry
+
+    lax.fori_loop(0, seqs, dispatch, 0)
+
+    s_copies = [remote(st.at[me], st.at[me], s_s.at[d - 1], s_r.at[d - 1], lax.rem(t + d, NT), e) for d in range(1, NT)]
+    for c in s_copies:
+        c.start()
+    y_tok = z * NY + oy
+    y_copies = {}
+    for d in (1, 2, 3, 0):
+        zz = zpeer(d)
+        psend[zz] = part[oy * NZ + zz].astype(BF16)
+        y_copies[d] = remote(psend.at[zz], yrecv.at[zz], y_s.at[d], y_r.at[d], y_tok, e)
+        y_copies[d].start()
+    for c in s_copies:
+        c.wait()
+    peaks = [st[r] for r in range(NT)]
+    top = functools.reduce(jnp.maximum, peaks)
+    total = jnp.zeros_like(top)
+    for r in range(NT):
+        total += pltpu.roll(peaks[r], 64, 1) * jnp.exp(peaks[r] - top)
+    for i, r in enumerate((me, oy * NZ + z)):
+        mine = st[r]
+        w = pltpu.roll(mine, 64, 1) * jnp.exp(mine - top) / total
+        for s in range(seqs):
+            wrow[i, pl.ds(s, own_w, stride=seqs), :] = jnp.broadcast_to(w[:, s:s + 1], (own_w, LANES))
+
+    z_copies = []
+    for d in (1, 2, 3, 0):
+        zz = zpeer(d)
+        y_copies[d].wait()
+        both = part[y * NZ + zz] * wrow[0] + yrecv[zz].astype(F32) * wrow[1]
+        if d:
+            zsend[zz] = both.astype(BF16)
+            c = remote(zsend.at[zz], zrecv.at[d - 1], z_s.at[d - 1], z_r.at[d - 1], zz * NY + y, e)
+            c.start()
+            z_copies.append(c)
+        else:
+            facc[...] = both
+    for c in z_copies:
+        c.wait()
+    xs[me] = (facc[...] + zrecv[0].astype(F32) + zrecv[1].astype(F32) + zrecv[2].astype(F32)).astype(BF16)
+
+    def gather(block, zs, zr, ys, yr):
+        zc = [remote(block(me), block(me), zs.at[d - 1], zr.at[d - 1], zpeer(d) * NY + y, e) for d in range(1, NZ)]
+        yc = [remote(block(me), block(me), ys.at[0], yr.at[0], y_tok, e)]
+        for c in zc:
+            c.start()
+        yc[0].start()
+        for d in range(1, NZ):
+            zc[d - 1].wait_recv()
+            got = y * NZ + lax.rem(z + NZ - d, NZ)
+            c = remote(block(got), block(got), ys.at[d], yr.at[d], y_tok, e)
+            c.start()
+            yc.append(c)
+        for c in zc:
+            c.wait_send()
+        for c in yc:
+            c.wait()
+
+    gather(lambda r: xs.at[r], az_s, az_r, ay_s, ay_r)
+
+    upper = lax.broadcasted_iota(jnp.int32, (pair_rows, 1), 0) < half_rows
+
+    def by_copy(d):
+        zz = zpeer(d)
+        return remote(bsend.at[zz], byrecv.at[zz], by_s.at[d], by_r.at[d], y_tok, e)
+
+    def bz_copy(d):
+        zz = zpeer(d)
+        return remote(bzsend.at[zz], bzrecv.at[d - 1], bz_s.at[d - 1], bz_r.at[d - 1], zz * NY + y, e)
+
+    def expert_pair(i, carry):
+        d = lax.rem(i + 1, NZ)
+        zz = zpeer(d)
+        first = i < NZ
+        p = jnp.where(first, oy, y) * NZ + zz
+        for c in w_copies(p):
+            c.wait()
+        rows = pl.ds(pl.multiple_of(p * pair_rows, 16), pair_rows)
+        x = jnp.concatenate([xs[k, rows, :] for k in range(NT)], axis=1)
+        h0 = jnp.dot(x, win[2 * p], preferred_element_type=F32)
+        h1 = jnp.dot(x, win[2 * p + 1], preferred_element_type=F32)
+        hid = gelu(jnp.where(upper, h0, h1))
+        zero = jnp.zeros_like(hid)
+        u0 = jnp.where(upper, hid, zero).astype(BF16)
+        u1 = jnp.where(upper, zero, hid).astype(BF16)
+        acc[...] = (jnp.dot(u0, wout[2 * p], preferred_element_type=F32)
+                    + jnp.dot(u1, wout[2 * p + 1], preferred_element_type=F32))
+
+        @pl.when(first)
+        def _():
+            bsend[zz] = acc[...].astype(BF16)
+            by_copy(d).start()
+
+        @pl.when(jnp.logical_not(first))
+        def _():
+            by_copy(d).wait()
+            acc[...] += byrecv[zz].astype(F32)
+
+            @pl.when(i < 2 * NZ - 1)
+            def _():
+                bzsend[zz] = acc[...].astype(BF16)
+                bz_copy(d).start()
+
+        return carry
+
+    lax.fori_loop(0, NT, expert_pair, 0)
+
+    for d in range(1, NZ):
+        bz_copy(d).wait()
+    done = (acc[...] + bzrecv[0].astype(F32) + bzrecv[1].astype(F32) + bzrecv[2].astype(F32)).astype(BF16)
+    for k in range(NE):
+        fin[k] = done[:, k * feat:(k + 1) * feat]
+    c_copies = []
+    for d in range(1, NE):
+        to = lax.rem(e + d, NE)
+        c = remote(fin.at[to], g.at[e, me], c_s.at[d - 1], c_r.at[d - 1], t, to)
+        c.start()
+        c_copies.append(c)
+    g[e, me] = fin[e]
+    for c in c_copies:
+        c.wait()
+    gather(lambda r: g.at[:, r], gz_s, gz_r, gy_s, gy_r)
+    out = pltpu.make_async_copy(g, g_hbm, gsem)
+    out.start()
+    for s in range(seqs):
+        cw_copy(s).wait()
+    out.wait()
+
+
+def combine_kernel(cw_ref, g_ref, o_ref, wide):
+    s = pl.program_id(0)
+    slots = cw_ref.shape[1]
+    tiles, rows, _ = wide.shape
+    seqs = rows // slots
+
+    @pl.when(s == 0)
+    def _():
+        for c in range(tiles):
+            wide[c] = g_ref[:, c * LANES:(c + 1) * LANES].astype(F32)
+
+    vals = jnp.concatenate([wide[c, pl.ds(s, slots, stride=seqs), :] for c in range(tiles)], axis=1).astype(BF16)
+    o_ref[0] = lax.dot_general(cw_ref[0], vals, (((0,), (0,)), ((), ())), preferred_element_type=F32).astype(BF16)
+
+
+def fused(tokens, slot_params, w_in, w_out):
+    seqs, length, width = tokens.shape
+    own_w = slot_params.shape[1]
+    slots = own_w * NE
+    experts, _, ff = w_in.shape
+    rows = seqs * own_w
+    pair_rows = rows // NT
+    feat = width // NE
+    dma = pltpu.SemaphoreType.DMA
+    any_spec = pl.BlockSpec(memory_space=pl.ANY)
+    cw, g = pl.pallas_call(
+        main_kernel,
+        out_shape=(jax.ShapeDtypeStruct((seqs, slots, length), BF16),
+                   jax.ShapeDtypeStruct((NE, NT, pair_rows, feat), BF16)),
+        in_specs=[any_spec, pl.BlockSpec(memory_space=pltpu.VMEM), any_spec, any_spec],
+        out_specs=(any_spec, any_spec),
+        scratch_shapes=[
+            pltpu.VMEM((3, length, width), BF16),
+            pltpu.VMEM((slots, width), BF16),
+            pltpu.VMEM((experts, width, ff), BF16),
+            pltpu.VMEM((experts, ff, width), BF16),
+            pltpu.VMEM((slots, length), F32),
+            pltpu.VMEM((seqs, slots, length), BF16),
+            pltpu.VMEM((NT, rows, LANES), F32),
+            pltpu.VMEM((NZ, rows, LANES), BF16),
+            pltpu.VMEM((NT, own_w, LANES), F32),
+            pltpu.VMEM((2, rows, LANES), F32),
+            pltpu.VMEM((NZ, rows, LANES), BF16),
+            pltpu.VMEM((NZ, rows, LANES), BF16),
+            pltpu.VMEM((NZ - 1, rows, LANES), BF16),
+            pltpu.VMEM((rows, LANES), F32),
+            pltpu.VMEM((NT, rows, LANES), BF16),
+            pltpu.VMEM((pair_rows, width), F32),
+            pltpu.VMEM((NZ, pair_rows, width), BF16),
+            pltpu.VMEM((NZ, pair_rows, width), BF16),
+            pltpu.VMEM((NZ, pair_rows, width), BF16),
+            pltpu.VMEM((NZ - 1, pair_rows, width), BF16),
+            pltpu.VMEM((NE, pair_rows, feat), BF16),
+            pltpu.VMEM((NE, NT, pair_rows, feat), BF16),
+            dma((3,)), dma((2, NT)), dma((seqs,)), dma,
+            dma((NE - 1,)), dma((NE - 1,)),
+            dma((NT - 1,)), dma((NT - 1,)),
+            dma((NZ,)), dma((NZ,)),
+            dma((NZ - 1,)), dma((NZ - 1,)),
+            dma((NZ - 1,)), dma((NZ - 1,)),
+            dma((NZ,)), dma((NZ,)),
+            dma((NZ,)), dma((NZ,)),
+            dma((NZ - 1,)), dma((NZ - 1,)),
+            dma((NE - 1,)), dma((NE - 1,)),
+            dma((NZ - 1,)), dma((NZ - 1,)),
+            dma((NZ,)), dma((NZ,)),
+        ],
+        compiler_params=pltpu.CompilerParams(collective_id=0, has_side_effects=True, vmem_limit_bytes=60 << 20),
+        name="dispatch_experts",
+    )(tokens, slot_params.T, w_in, w_out)
+    return pl.pallas_call(
+        combine_kernel,
+        grid=(seqs,),
+        out_shape=jax.ShapeDtypeStruct((seqs, length, feat), BF16),
+        in_specs=[pl.BlockSpec((1, slots, length), lambda s: (s, 0, 0)),
+                  pl.BlockSpec((slots * seqs, feat), lambda s: (0, 0))],
+        out_specs=pl.BlockSpec((1, length, feat), lambda s: (s, 0, 0)),
+        scratch_shapes=[pltpu.VMEM((feat // LANES, slots * seqs, LANES), F32)],
+        compiler_params=pltpu.CompilerParams(vmem_limit_bytes=32 << 20),
+        name="combine",
+    )(cw, g.reshape(slots * seqs, feat))
 
 
 def shards(tokens, slot_params, w_in, w_out):
@@ -38,8 +351,9 @@
 
 
 def solution(mesh):
+    quick = mesh.shape["tok"] == NT and mesh.shape["exp"] == NE
     return jax.shard_map(
-        shards,
+        fused if quick else shards,
         mesh=mesh,
         in_specs=(
             P(None, "tok", None),

time: 547 us -> 107 us (0.20)
  blocking collectives: 383 us -> 0 us
  Pallas kernels: 0 us -> 103 us
  waiting for transfers between devices: 66.6 us -> 0 us
  matrix products: 50.8 us -> 0 us
  local copies, waits for them, and re-layouts: 22.2 us -> 3.02 us
  between operations: 14.9 us -> 0.02 us
  other arithmetic: 9.19 us -> 0 us
    psum x2 -> x0, blocking collectives: 345 us -> none  [the longest x1 327 us: shards(): summed = lax.psum(partial_out, 'tok').astype(jnp.bfloat16)]
    pallas_call x0 -> x2, Pallas kernels: none -> 103 us  [the longest x1 96 us: fused(): pl.pallas_call(main_kernel, out_shape=(jax.ShapeDtypeStruct((seqs, slots,...]
    psum x1 -> x0, waiting for transfers between devices: 66 us -> none  [shards(): slot_sum, slot_den = lax.psum((local_sum, local_den), 'tok')]
    dot_general x5 -> x0, matrix products: 50.8 us -> none  [the longest x1 12.3 us: shards(): jnp.einsum('std,dj->sjt', tokens, slot_params, preferred_element_type=jnp...]
    pmax x1 -> x0, blocking collectives: 23.4 us -> none  [shards(): slot_peak = lax.pmax(local_max, 'tok')]
    all_to_all x1 -> x0, blocking collectives: 14.2 us -> none  [shards(): lax.all_to_all(summed, 'exp', split_axis=2, concat_axis=1, tiled=True)]
    unnamed x8 -> x4, local copies, waits for them, and re-layouts: 9.98 us -> 3.02 us
    reshape x2 -> x0, local copies, waits for them, and re-layouts: 6.96 us -> none  [the longest x1 6.51 us: shards(): partial_out = partial_out.reshape(seq_count, own_width, width)]
  transfers between devices with their start and end apart: 2 -> 0, of which waited for: 1 -> 0; matrix products, arithmetic and copies ran while one was open for 8% -> 0% of each run, Pallas kernels for 0% -> 0%
where the time goes in v1:
time: 107 us; the launch traced here: 106 us
  Pallas kernels  103 us (96%)
  local copies, waits for them, and re-layouts  3.02 us (3%)
    pallas_call x1, Pallas kernels, fused(): pl.pallas_call(main_kernel, out_shape=(jax.ShapeDtypeStruct((seqs, slots,...  96 us
    pallas_call x1, Pallas kernels, fused(): pl.pallas_call(combine_kernel, grid=(seqs,), out_shape=jax.ShapeDtypeStru...  7.14 us
    unnamed x4, local copies, waits for them, and re-layouts  3.02 us

profile of v1, /device:TPU:0, one launch (start us, length us, event | category | flops | bytes accessed | tf_op | source)
XLA Modules:
  0.0 106.2 jit_solution(15037196646071502687)
XLA Ops:
  0.0 96.0 %dispatch_experts.1 = (bf16[12,128,1024]{2,1,0:T(8,128)(2,1)}, bf16[4,8,48,256]{3,2,1,0:T(8,128)(2,1)}) custom-call(bf16[12,1024,1024]{2,1,0:T(8,128)(2,1)} %tok_hbm.1, bf16[32,1024]{1,0:T(8,128)(2,1)} %bitcast.3, bf16[16,1024,512]{2,1,0:T(8,128)(2,1)} %win_hbm.1, bf16[16,512,1024]{2,1,0:T(8,128)(2,1)} %wout_hbm.1), custom_call_target="tpu_custom_call" | custom-call | tf_op jit(solution)/shard_map/dispatch_experts/pallas_call | solution.py:264
  96.1 0.0 copy-start
  96.1 1.9 %copy-done = bf16[12,128,1024]{2,1,0:T(8,128)(2,1)S(1)} copy-done((bf16[12,128,1024]{2,1,0:T(8,128)(2,1)S(1)}, bf16[12,128,1024]{2,1,0:T(8,128)(2,1)}, u32[]{:S(2)}) %copy-start) | copy-done | bytes 3145752
  97.9 0.0 copy-start.1
  97.9 1.1 %copy-done.1 = bf16[4,8,48,256]{3,2,1,0:T(8,128)(2,1)S(1)} copy-done((bf16[4,8,48,256]{3,2,1,0:T(8,128)(2,1)S(1)}, bf16[4,8,48,256]{3,2,1,0:T(8,128)(2,1)}, u32[]{:S(2)}) %copy-start.1) | copy-done | bytes 786456
  99.1 7.1 %combine.1 = bf16[12,1024,256]{2,1,0:T(8,128)(2,1)} custom-call(bf16[12,128,1024]{2,1,0:T(8,128)(2,1)S(1)} %copy-done, bf16[1536,256]{1,0:T(8,128)(2,1)S(1)} %bitcast.2), custom_call_target="tpu_custom_call" | custom-call | tf_op jit(solution)/shard_map/combine/pallas_call | solution.py:309
Async XLA Ops:
  96.1 1.9 %copy-start = (bf16[12,128,1024]{2,1,0:T(8,128)(2,1)S(1)}, bf16[12,128,1024]{2,1,0:T(8,128)(2,1)}, u32[]{:S(2)}) copy-start(bf16[12,128,1024]{2,1,0:T(8,128)(2,1)} %get-tuple-element.7.cw_ref) | copy-start | bytes 9437188
  97.9 1.1 %copy-start.1 = (bf16[4,8,48,256]{3,2,1,0:T(8,128)(2,1)S(1)}, bf16[4,8,48,256]{3,2,1,0:T(8,128)(2,1)}, u32[]{:S(2)}) copy-start(bf16[4,8,48,256]{3,2,1,0:T(8,128)(2,1)} %get-tuple-element.8) | copy-start | bytes 2359300

commit v2 on v1

--- a/solution.py
+++ b/solution.py
@@ -11,6 +11,7 @@
 NZ, NY = 4, 2
 NT = NZ * NY
 NE = 4
+NG = 3
 LANES = 128
 MESH = pl.DeviceIdType.MESH
 F32, BF16 = jnp.float32, jnp.bfloat16
@@ -26,12 +27,14 @@
     acc, bsend, byrecv, bzsend, bzrecv, fin, g,
     tsem, wsem, cwsem, gsem,
     p_s, p_r, s_s, s_r, y_s, y_r, z_s, z_r, az_s, az_r, ay_s, ay_r,
-    by_s, by_r, bz_s, bz_r, c_s, c_r, gz_s, gz_r, gy_s, gy_r,
+    by_s, by_r, bz_s, bz_r, c_s, c_r, gl_s, gl_r, gr_s, gr_r, gy_s, gy_r,
 ):
     seqs, _, width = tok_hbm.shape
     own_w = prm_ref.shape[0]
     pair_rows = acc.shape[0]
-    half_rows = pair_rows // 2
+    group = seqs // NG
+    own_rows = own_w * group
+    pair_part = pair_rows // NG
     feat = g.shape[3]
     t = lax.axis_index("tok")
     e = lax.axis_index("exp")
@@ -73,7 +76,8 @@
     for c in p_copies:
         c.start()
     prm[own_cols, :] = prm_ref[...]
-    st[me] = jnp.ones((own_w, LANES), F32)
+    for i in range(NG):
+        st[i, me] = jnp.ones((own_w, LANES), F32)
     for c in p_copies:
         c.wait()
 
@@ -84,13 +88,14 @@
         def _():
             tok_copy(s + 2).start()
 
-        @pl.when(s < NT)
-        def _():
-            for c in w_copies(s):
+        @pl.when(s >= seqs - NT)
+        def _():
+            for c in w_copies(s - (seqs - NT)):
                 c.start()
 
         tok_copy(s).wait()
         slot = lax.rem(s, 3)
+        gi, in_group = s // group, lax.rem(s, group)
         logits = lax.dot_general(prm[...], tbuf[slot], (((1,), (1,)), ((), ())), preferred_element_type=F32)
         lg[...] = logits
         ex = jnp.exp(logits - jnp.max(logits, axis=0, keepdims=True))
@@ -103,71 +108,104 @@
         ssum = jnp.dot(dx.astype(BF16), tbuf[slot], preferred_element_type=F32)
         scaled = ssum / den
         for k in range(NT):
-            part[k, pl.ds(s, own_w, stride=seqs), :] = scaled[:, k * LANES:(k + 1) * LANES]
-        st[me] = jnp.where(lane == s, peak, jnp.where(lane == s + 64, den, st[me]))
+            part[k, gi, pl.ds(in_group, own_w, stride=group), :] = scaled[:, k * LANES:(k + 1) * LANES]
+        st[gi, me] = jnp.where(lane == in_group, peak, jnp.where(lane == in_group + 64, den, st[gi, me]))
         return carry
 
-    lax.fori_loop(0, seqs, dispatch, 0)
-
-    s_copies = [remote(st.at[me], st.at[me], s_s.at[d - 1], s_r.at[d - 1], lax.rem(t + d, NT), e) for d in range(1, NT)]
-    for c in s_copies:
+    y_tok = z * NY + oy
+    flight = {}
+
+    def send_partial(i):
+        stats = [remote(st.at[i, me], st.at[i, me], s_s.at[i, d - 1], s_r.at[i, d - 1], lax.rem(t + d, NT), e) for d in range(1, NT)]
+        for c in stats:
+            c.start()
+        for zz in range(NZ):
+            psend[i, zz] = part[oy * NZ + zz, i].astype(BF16)
+        c = remote(psend.at[i], yrecv.at[i], y_s.at[i], y_r.at[i], y_tok, e)
         c.start()
-    y_tok = z * NY + oy
-    y_copies = {}
-    for d in (1, 2, 3, 0):
-        zz = zpeer(d)
-        psend[zz] = part[oy * NZ + zz].astype(BF16)
-        y_copies[d] = remote(psend.at[zz], yrecv.at[zz], y_s.at[d], y_r.at[d], y_tok, e)
-        y_copies[d].start()
-    for c in s_copies:
-        c.wait()
-    peaks = [st[r] for r in range(NT)]
-    top = functools.reduce(jnp.maximum, peaks)
-    total = jnp.zeros_like(top)
-    for r in range(NT):
-        total += pltpu.roll(peaks[r], 64, 1) * jnp.exp(peaks[r] - top)
-    for i, r in enumerate((me, oy * NZ + z)):
-        mine = st[r]
-        w = pltpu.roll(mine, 64, 1) * jnp.exp(mine - top) / total
-        for s in range(seqs):
-            wrow[i, pl.ds(s, own_w, stride=seqs), :] = jnp.broadcast_to(w[:, s:s + 1], (own_w, LANES))
-
-    z_copies = []
-    for d in (1, 2, 3, 0):
-        zz = zpeer(d)
-        y_copies[d].wait()
-        both = part[y * NZ + zz] * wrow[0] + yrecv[zz].astype(F32) * wrow[1]
-        if d:
-            zsend[zz] = both.astype(BF16)
-            c = remote(zsend.at[zz], zrecv.at[d - 1], z_s.at[d - 1], z_r.at[d - 1], zz * NY + y, e)
-            c.start()
-            z_copies.append(c)
-        else:
-            facc[...] = both
-    for c in z_copies:
-        c.wait()
-    xs[me] = (facc[...] + zrecv[0].astype(F32) + zrecv[1].astype(F32) + zrecv[2].astype(F32)).astype(BF16)
-
-    def gather(block, zs, zr, ys, yr):
-        zc = [remote(block(me), block(me), zs.at[d - 1], zr.at[d - 1], zpeer(d) * NY + y, e) for d in range(1, NZ)]
-        yc = [remote(block(me), block(me), ys.at[0], yr.at[0], y_tok, e)]
+        flight[i] = stats + [c]
+
+    def reduce_y(i):
+        for c in flight[i]:
+            c.wait()
+        peaks = [st[i, r] for r in range(NT)]
+        top = functools.reduce(jnp.maximum, peaks)
+        total = jnp.zeros_like(top)
+        for r in range(NT):
+            total += pltpu.roll(peaks[r], 64, 1) * jnp.exp(peaks[r] - top)
+        for n, r in enumerate((me, oy * NZ + z)):
+            mine = st[i, r]
+            w = pltpu.roll(mine, 64, 1) * jnp.exp(mine - top) / total
+            for q in range(group):
+                wrow[n, pl.ds(q, own_w, stride=group), :] = jnp.broadcast_to(w[:, q:q + 1], (own_w, LANES))
+        copies = []
+        for d in (1, 2, 3, 0):
+            zz = zpeer(d)
+            both = part[y * NZ + zz, i] * wrow[0] + yrecv[i, zz].astype(F32) * wrow[1]
+            if d:
+                zsend[i, zz] = both.astype(BF16)
+                c = remote(zsend.at[i, zz], zrecv.at[i, d - 1], z_s.at[i, d - 1], z_r.at[i, d - 1], zz * NY + y, e)
+                c.start()
+                copies.append(c)
+            else:
+                facc[i] = both
+        flight[i] = copies
+
+    def finish_z(i):
+        for c in flight[i]:
+            c.wait()
+        xs[i, me] = (facc[i] + zrecv[i, 0].astype(F32) + zrecv[i, 1].astype(F32) + zrecv[i, 2].astype(F32)).astype(BF16)
+        zc = [remote(xs.at[i, me], xs.at[i, me], az_s.at[i, d - 1], az_r.at[i, d - 1], zpeer(d) * NY + y, e) for d in range(1, NZ)]
+        yc = remote(xs.at[i, me], xs.at[i, me], ay_s.at[i, 0], ay_r.at[i, 0], y_tok, e)
         for c in zc:
             c.start()
-        yc[0].start()
+        yc.start()
+        flight[i] = (zc, [yc])
+
+    def forward(i):
+        zc, yc = flight[i]
         for d in range(1, NZ):
             zc[d - 1].wait_recv()
             got = y * NZ + lax.rem(z + NZ - d, NZ)
-            c = remote(block(got), block(got), ys.at[d], yr.at[d], y_tok, e)
+            c = remote(xs.at[i, got], xs.at[i, got], ay_s.at[i, d], ay_r.at[i, d], y_tok, e)
             c.start()
             yc.append(c)
+
+    def settle(i):
+        zc, yc = flight[i]
         for c in zc:
             c.wait_send()
         for c in yc:
             c.wait()
 
-    gather(lambda r: xs.at[r], az_s, az_r, ay_s, ay_r)
-
-    upper = lax.broadcasted_iota(jnp.int32, (pair_rows, 1), 0) < half_rows
+    half = group // 2
+
+    def run(i):
+        lax.fori_loop(i * half, (i + 1) * half, dispatch, 0)
+
+    run(0)
+    run(1)
+    send_partial(0)
+    run(2)
+    reduce_y(0)
+    run(3)
+    finish_z(0)
+    send_partial(1)
+    run(4)
+    reduce_y(1)
+    forward(0)
+    run(5)
+    send_partial(2)
+    finish_z(1)
+    reduce_y(2)
+    forward(1)
+    finish_z(2)
+    settle(0)
+    forward(2)
+    settle(1)
+    settle(2)
+
+    upper = lax.rem(lax.broadcasted_iota(jnp.int32, (pair_rows, 1), 0), pair_part) < pair_part // 2
 
     def by_copy(d):
         zz = zpeer(d)
@@ -184,8 +222,8 @@
         p = jnp.where(first, oy, y) * NZ + zz
         for c in w_copies(p):
             c.wait()
-        rows = pl.ds(pl.multiple_of(p * pair_rows, 16), pair_rows)
-        x = jnp.concatenate([xs[k, rows, :] for k in range(NT)], axis=1)
+        rows = pl.ds(pl.multiple_of(p * pair_part, 16), pair_part)
+        x = jnp.concatenate([jnp.concatenate([xs[i, k, rows, :] for k in range(NT)], axis=1) for i in range(NG)], axis=0)
         h0 = jnp.dot(x, win[2 * p], preferred_element_type=F32)
         h1 = jnp.dot(x, win[2 * p + 1], preferred_element_type=F32)
         hid = gelu(jnp.where(upper, h0, h1))
@@ -228,7 +266,59 @@
     g[e, me] = fin[e]
     for c in c_copies:
         c.wait()
-    gather(lambda r: g.at[:, r], gz_s, gz_r, gy_s, gy_r)
+
+    def block(zz):
+        return g.at[:, y * NZ + zz]
+
+    def hop(zz, sems, n, step):
+        to = jnp.clip(z + step, 0, NZ - 1) * NY + y
+        return remote(block(zz), block(zz), sems[0].at[n], sems[1].at[n], to, e)
+
+    def cross(zz, n):
+        return remote(block(zz), block(zz), gy_s.at[n], gy_r.at[n], y_tok, e)
+
+    ways = ((1, (gr_s, gr_r), 0), (-1, (gl_s, gl_r), NZ - 1))
+    for step, sems, off in ways:
+        @pl.when(z != NZ - 1 if step == 1 else z != 0)
+        def _():
+            hop(z, sems, 0, step).start()
+    cross(z, 0).start()
+    for n in range(1, NZ):
+        for step, sems, off in ways:
+            zz = z - step * n
+            inside = zz >= 0 if step == 1 else zz < NZ
+            at = jnp.clip(zz, 0, NZ - 1)
+            more = jnp.logical_and(inside, z != NZ - 1 if step == 1 else z != 0)
+
+            @pl.when(inside)
+            def _():
+                hop(at, sems, n - 1, -step).wait_recv()
+                cross(at, off + n).start()
+
+            if n < NZ - 1:
+                @pl.when(more)
+                def _():
+                    hop(at, sems, n, step).start()
+    for step, sems, off in ways:
+        @pl.when(z != NZ - 1 if step == 1 else z != 0)
+        def _():
+            hop(z, sems, 0, step).wait_send()
+    cross(z, 0).wait()
+    for n in range(1, NZ):
+        for step, sems, off in ways:
+            zz = z - step * n
+            inside = zz >= 0 if step == 1 else zz < NZ
+            at = jnp.clip(zz, 0, NZ - 1)
+            more = jnp.logical_and(inside, z != NZ - 1 if step == 1 else z != 0)
+
+            @pl.when(inside)
+            def _():
+                cross(at, off + n).wait()
+
+            if n < NZ - 1:
+                @pl.when(more)
+                def _():
+                    hop(at, sems, n, step).wait_send()
     out = pltpu.make_async_copy(g, g_hbm, gsem)
     out.start()
     for s in range(seqs):
@@ -237,18 +327,24 @@
 
 
 def combine_kernel(cw_ref, g_ref, o_ref, wide):
-    s = pl.program_id(0)
-    slots = cw_ref.shape[1]
-    tiles, rows, _ = wide.shape
-    seqs = rows // slots
-
-    @pl.when(s == 0)
+    seqs_here, slots, _ = cw_ref.shape
+    tiles, groups, _, _ = wide.shape
+    blocks = g_ref.shape[0]
+    span = g_ref.shape[1] // groups
+    size = pl.num_programs(0) * seqs_here // groups
+
+    @pl.when(pl.program_id(0) == 0)
     def _():
         for c in range(tiles):
-            wide[c] = g_ref[:, c * LANES:(c + 1) * LANES].astype(F32)
-
-    vals = jnp.concatenate([wide[c, pl.ds(s, slots, stride=seqs), :] for c in range(tiles)], axis=1).astype(BF16)
-    o_ref[0] = lax.dot_general(cw_ref[0], vals, (((0,), (0,)), ((), ())), preferred_element_type=F32).astype(BF16)
+            for i in range(groups):
+                part = g_ref[:, i * span:(i + 1) * span, c * LANES:(c + 1) * LANES]
+                wide[c, i] = part.astype(F32).reshape(blocks * span, LANES)
+
+    for n in range(seqs_here):
+        s = pl.program_id(0) * seqs_here + n
+        i, q = s // size, lax.rem(s, size)
+        vals = jnp.concatenate([wide[c, i, pl.ds(q, slots, stride=size), :] for c in range(tiles)], axis=1).astype(BF16)
+        o_ref[n] = lax.dot_general(cw_ref[n], vals, (((0,), (0,)), ((), ())), preferred_element_type=F32).astype(BF16)
 
 
 def fused(tokens, slot_params, w_in, w_out):
@@ -258,6 +354,8 @@
     experts, _, ff = w_in.shape
     rows = seqs * own_w
     pair_rows = rows // NT
+    own_rows = rows // NG
+    step = 2
     feat = width // NE
     dma = pltpu.SemaphoreType.DMA
     any_spec = pl.BlockSpec(memory_space=pl.ANY)
@@ -274,15 +372,15 @@
             pltpu.VMEM((experts, ff, width), BF16),
             pltpu.VMEM((slots, length), F32),
             pltpu.VMEM((seqs, slots, length), BF16),
-            pltpu.VMEM((NT, rows, LANES), F32),
-            pltpu.VMEM((NZ, rows, LANES), BF16),
-            pltpu.VMEM((NT, own_w, LANES), F32),
-            pltpu.VMEM((2, rows, LANES), F32),
-            pltpu.VMEM((NZ, rows, LANES), BF16),
-            pltpu.VMEM((NZ, rows, LANES), BF16),
-            pltpu.VMEM((NZ - 1, rows, LANES), BF16),
-            pltpu.VMEM((rows, LANES), F32),
-            pltpu.VMEM((NT, rows, LANES), BF16),
+            pltpu.VMEM((NT, NG, own_rows, LANES), F32),
+            pltpu.VMEM((NG, NZ, own_rows, LANES), BF16),
+            pltpu.VMEM((NG, NT, own_w, LANES), F32),
+            pltpu.VMEM((2, own_rows, LANES), F32),
+            pltpu.VMEM((NG, NZ, own_rows, LANES), BF16),
+            pltpu.VMEM((NG, NZ, own_rows, LANES), BF16),
+            pltpu.VMEM((NG, NZ - 1, own_rows, LANES), BF16),
+            pltpu.VMEM((NG, own_rows, LANES), F32),
+            pltpu.VMEM((NG, NT, own_rows, LANES), BF16),
             pltpu.VMEM((pair_rows, width), F32),
             pltpu.VMEM((NZ, pair_rows, width), BF16),
             pltpu.VMEM((NZ, pair_rows, width), BF16),
@@ -292,31 +390,32 @@
             pltpu.VMEM((NE, NT, pair_rows, feat), BF16),
             dma((3,)), dma((2, NT)), dma((seqs,)), dma,
             dma((NE - 1,)), dma((NE - 1,)),
-            dma((NT - 1,)), dma((NT - 1,)),
-            dma((NZ,)), dma((NZ,)),
-            dma((NZ - 1,)), dma((NZ - 1,)),
-            dma((NZ - 1,)), dma((NZ - 1,)),
-            dma((NZ,)), dma((NZ,)),
+            dma((NG, NT - 1)), dma((NG, NT - 1)),
+            dma((NG,)), dma((NG,)),
+            dma((NG, NZ - 1)), dma((NG, NZ - 1)),
+            dma((NG, NZ - 1)), dma((NG, NZ - 1)),
+            dma((NG, NZ)), dma((NG, NZ)),
             dma((NZ,)), dma((NZ,)),
             dma((NZ - 1,)), dma((NZ - 1,)),
             dma((NE - 1,)), dma((NE - 1,)),
             dma((NZ - 1,)), dma((NZ - 1,)),
-            dma((NZ,)), dma((NZ,)),
+            dma((NZ - 1,)), dma((NZ - 1,)),
+            dma((2 * NZ - 1,)), dma((2 * NZ - 1,)),
         ],
         compiler_params=pltpu.CompilerParams(collective_id=0, has_side_effects=True, vmem_limit_bytes=60 << 20),
         name="dispatch_experts",
     )(tokens, slot_params.T, w_in, w_out)
     return pl.pallas_call(
         combine_kernel,
-        grid=(seqs,),
+        grid=(seqs // step,),
         out_shape=jax.ShapeDtypeStruct((seqs, length, feat), BF16),
-        in_specs=[pl.BlockSpec((1, slots, length), lambda s: (s, 0, 0)),
-                  pl.BlockSpec((slots * seqs, feat), lambda s: (0, 0))],
-        out_specs=pl.BlockSpec((1, length, feat), lambda s: (s, 0, 0)),
-        scratch_shapes=[pltpu.VMEM((feat // LANES, slots * seqs, LANES), F32)],
-        compiler_params=pltpu.CompilerParams(vmem_limit_bytes=32 << 20),
+        in_specs=[pl.BlockSpec((step, slots, length), lambda s: (s, 0, 0)),
+                  pl.BlockSpec((NE * NT, pair_rows, feat), lambda s: (0, 0, 0))],
+        out_specs=pl.BlockSpec((step, length, feat), lambda s: (s, 0, 0)),
+        scratch_shapes=[pltpu.VMEM((feat // LANES, NG, slots * seqs // NG, LANES), F32)],
+        compiler_params=pltpu.CompilerParams(vmem_limit_bytes=60 << 20),
         name="combine",
-    )(cw, g.reshape(slots * seqs, feat))
+    )(cw, g.reshape(NE * NT, pair_rows, feat))
 
 
 def shards(tokens, slot_params, w_in, w_out):

time: 107 us -> 95.8 us (0.90)
  Pallas kernels: 103 us -> 95.5 us
  local copies, waits for them, and re-layouts: 3.02 us -> 0 us
    pallas_call x1, Pallas kernels: 96 us -> 88.2 us  [fused(): pl.pallas_call(main_kernel, out_shape=(jax.ShapeDtypeStruct((seqs, slots,...]
    unnamed x4 -> x0, local copies, waits for them, and re-layouts: 3.02 us -> none
where the time goes in v2:
time: 95.8 us; the launch traced here: 95.5 us
  Pallas kernels  95.5 us (100%)
    pallas_call x1, Pallas kernels, fused(): pl.pallas_call(main_kernel, out_shape=(jax.ShapeDtypeStruct((seqs, slots,...  88.2 us
    pallas_call x1, Pallas kernels, fused(): pl.pallas_call(combine_kernel, grid=(seqs // step,), out_shape=jax.ShapeD...  7.3 us

profile of v2, /device:TPU:0, one launch (start us, length us, event | category | flops | bytes accessed | tf_op | source)
XLA Modules:
  0.0 95.5 jit_solution(11262529024658679997)
XLA Ops:
  0.0 88.2 %dispatch_experts.1 = (bf16[12,128,1024]{2,1,0:T(8,128)(2,1)}, bf16[4,8,48,256]{3,2,1,0:T(8,128)(2,1)}) custom-call(bf16[12,1024,1024]{2,1,0:T(8,128)(2,1)} %tok_hbm.1, bf16[32,1024]{1,0:T(8,128)(2,1)} %bitcast.3, bf16[16,1024,512]{2,1,0:T(8,128)(2,1)} %win_hbm.1, bf16[16,512,1024]{2,1,0:T(8,128)(2,1)} %wout_hbm.1), custom_call_target="tpu_custom_call" | custom-call | tf_op jit(solution)/shard_map/dispatch_experts/pallas_call | solution.py:362
  88.2 7.3 %combine.1 = bf16[12,1024,256]{2,1,0:T(8,128)(2,1)} custom-call(bf16[12,128,1024]{2,1,0:T(8,128)(2,1)} %get-tuple-element.7.cw_ref, bf16[32,48,256]{2,1,0:T(8,128)(2,1)} %bitcast.2), custom_call_target="tpu_custom_call" | custom-call | tf_op jit(solution)/shard_map/combine/pallas_call | solution.py:408
